TPU v7x, 32 devices: a whole 2x2x4 slice. The times are simulated.
32 devices in a mesh: groups: 2 (over x), seq: 16 (over z, y, core).
Axes of the slice: x: 2, y: 2, z: 4, core: 2. Of those that a mesh axis runs over, the one named last changes fastest.
Arguments:
- features: bfloat16 [4096, 2048], P(('groups', 'seq')), parts along dimension 0, may hold values from -40 to 40
- state_write: bfloat16 [4096, 64], P(('groups', 'seq')), parts along dimension 0, may hold values from -0.75 to 0.75
- state_read: bfloat16 [4096, 64], P(('groups', 'seq')), parts along dimension 0, may hold values from -0.75 to 0.75
- log_decay: float32 [4096, 32], P(('groups', 'seq')), parts along dimension 0, may hold values from -2 to 0
- skip_gain: float32 [32], replicated, may hold values from 1 to 4
- post_gain: float32 [2048], replicated, may hold values from 0.5 to 2
- start_index: int32 [4096], P(('groups', 'seq')), parts along dimension 0, may hold values from 0 to 2047, as said below
- step_noise: bfloat16 [3, 4096, 1024], P(None, ('groups', 'seq')), parts along dimension 1, may hold values from -4 to 4
- act_weight: bfloat16 [2048, 128], replicated, may hold values from -0.125 to 0.125
- dyn_weight: bfloat16 [2048, 1024], replicated, may hold values from -0.125 to 0.125
- act_in_weight: bfloat16 [128, 1024], replicated, may hold values from -0.5 to 0.5
- out_weight: bfloat16 [1024, 2048], replicated, may hold values from -0.1875 to 0.1875
- value_weight: bfloat16 [1024], replicated, may hold values from -0.1875 to 0.1875
Outputs:
- posterior: bfloat16 [4096, 2048], P(('groups', 'seq')), parts along dimension 0
- values: float32 [3, 4096], P(None, ('groups', 'seq')), parts along dimension 1
- final_latent: bfloat16 [4096, 2048], P(('groups', 'seq')), parts along dimension 0
There are 2 independent parts, one for each index of `groups`. A program takes and returns all parts, laid end to end along the dimension named above; an argument that names none is the same for every part. Nothing has to cross between parts.
Inputs may be any that keep to these rules, and one draw needn't show every extreme that they name: `start_index`: each aligned block of 128 starts (the starts of one device) names exactly 8 time steps in every aligned range of 128 time steps.
All inputs are finite; a program needn't handle non-finite values.
Results may differ from a plain program's by a relative error of at most 0.01.
Values may be sent and summed in bfloat16 or wider, within the bound.
No kernel may reach another device: no remote copies, remote signals or barrier semaphores. Data moves between devices by JAX's collectives and lax.ppermute only.
A program may use at most 192 MiB of HBM per device.

v0:
```python
import jax
import jax.numpy as jnp
from jax import lax
from jax.sharding import PartitionSpec as P


def entering(shard, axis, combine, identity):
    count, mine = (lax.axis_size(axis), lax.axis_index(axis))
    everything = jax.tree.map(lambda part: lax.all_gather(part, axis), shard)
    start = jax.tree.map(
        lambda part, zero: jnp.broadcast_to(jnp.asarray(zero, part.dtype), part.shape),
        shard,
        identity,
    )

    def lap(k, before):
        reached = k < mine
        new = combine(before, jax.tree.map(lambda part: part[k], everything))
        return jax.tree.map(lambda a, b: jnp.where(reached, a, b), new, before)

    return lax.fori_loop(0, count, lap, start)


def lower_ones(count):
    positions = jnp.arange(count, dtype=jnp.int32)
    return (positions[:, None] >= positions[None, :]).astype(jnp.float32)


def local_pass(wide_in, write_in, read_in, decay_in):
    row_count, width = wide_in.shape
    head_count = decay_in.shape[1]
    head_width = width // head_count
    block = min(256, row_count)
    block_count = row_count // block
    positions = jnp.arange(block, dtype=jnp.int32)
    lower_mask = positions[:, None] >= positions[None, :]
    lower_table = lower_mask.astype(jnp.float32)

    def advance(state_now, inputs):
        x_block, write_block, read_block, decay_block = inputs
        running = jnp.dot(lower_table, decay_block, precision=lax.Precision.HIGHEST)
        running_t = running.T
        spread = running_t[:, :, None] - running_t[:, None, :]
        weight = jnp.exp(jnp.where(lower_mask[None], spread, -jnp.inf))
        gram = jnp.dot(read_block, write_block.T, preferred_element_type=jnp.float32)
        inner_part = jnp.einsum(
            "hts,shp->thp",
            weight * gram[None],
            x_block.reshape(block, head_count, head_width),
            precision=lax.Precision.HIGHEST,
        ).reshape(block, width)
        read_wide = read_block.astype(jnp.float32)
        carried = jnp.dot(read_wide, state_now, precision=lax.Precision.HIGHEST) * jnp.repeat(
            jnp.exp(running), head_width, axis=1
        )
        tail = jnp.repeat(jnp.exp(running[-1:] - running), head_width, axis=1)
        whole_decay = jnp.repeat(jnp.exp(running[-1]), head_width)
        added = jnp.einsum(
            "sn,sd->nd",
            write_block.astype(jnp.float32),
            x_block * tail,
            precision=lax.Precision.HIGHEST,
        )
        state_next = state_now * whole_decay[None, :] + added
        return (state_next, inner_part + carried)

    zero_state = jnp.zeros((write_in.shape[1], width), jnp.float32)
    inputs = (
        wide_in.reshape(block_count, block, width),
        write_in.reshape(block_count, block, write_in.shape[1]),
        read_in.reshape(block_count, block, read_in.shape[1]),
        decay_in.reshape(block_count, block, head_count),
    )
    end_state, outputs = lax.scan(advance, zero_state, inputs)
    return (end_state, outputs.reshape(row_count, width))


def join_states(earlier, later):
    grow = jnp.repeat(later[0], earlier[1].shape[1] // later[0].shape[0])
    return (earlier[0] * later[0], earlier[1] * grow[None, :] + later[1])


def regroup_rows(posterior, start_index):
    row_count = posterior.shape[0]
    peer_count = lax.axis_size("seq")
    start_count = start_index.shape[0]
    slot_cap = start_count // peer_count
    owners = start_index // row_count
    offset = start_index % row_count
    owner_hits = (owners[:, None] == jnp.arange(peer_count, dtype=jnp.int32)[None, :]).astype(
        jnp.float32
    )
    running_hits = jnp.dot(lower_ones(start_count), owner_hits, precision=lax.Precision.HIGHEST)
    slot_rank = jnp.sum(running_hits * owner_hits, axis=1).astype(jnp.int32) - 1
    slot_index = owners * slot_cap + slot_rank
    wanted = (
        jnp.zeros((peer_count * slot_cap,), jnp.int32)
        .at[slot_index]
        .set(offset)
        .reshape(peer_count, slot_cap)
    )
    picked = jnp.take(
        posterior, lax.all_to_all(wanted, "seq", split_axis=0, concat_axis=0, tiled=True), axis=0
    )
    landed = lax.all_to_all(picked, "seq", split_axis=0, concat_axis=0, tiled=True)
    return jnp.take(landed.reshape(peer_count * slot_cap, posterior.shape[1]), slot_index, axis=0)


def imagine(latent, step_noise, act_weight, dyn_weight, act_in_weight, out_weight, value_weight):
    value_list = []
    for step_idx in range(step_noise.shape[0]):
        wide = latent.astype(jnp.float32)
        normed = (wide * lax.rsqrt(jnp.mean(wide * wide, axis=-1, keepdims=True) + 1e-06)).astype(
            jnp.bfloat16
        )
        action = jnp.tanh(jnp.dot(normed, act_weight, preferred_element_type=jnp.float32)).astype(
            jnp.bfloat16
        )
        inner = jnp.dot(normed, dyn_weight, preferred_element_type=jnp.float32) + jnp.dot(
            action, act_in_weight, preferred_element_type=jnp.float32
        )
        hidden = (jax.nn.silu(inner) + step_noise[step_idx].astype(jnp.float32)).astype(
            jnp.bfloat16
        )
        value_list.append(jnp.dot(hidden, value_weight, preferred_element_type=jnp.float32))
        latent = (wide + jnp.dot(hidden, out_weight, preferred_element_type=jnp.float32)).astype(
            jnp.bfloat16
        )
    return (jnp.stack(value_list), latent)


def per_device(
    features,
    state_write,
    state_read,
    log_decay,
    skip_gain,
    post_gain,
    start_index,
    step_noise,
    act_weight,
    dyn_weight,
    act_in_weight,
    out_weight,
    value_weight,
):
    row_count, width = features.shape
    head_count = log_decay.shape[1]
    head_width = width // head_count
    wide_in = features.astype(jnp.float32)
    end_state, local_out = local_pass(wide_in, state_write, state_read, log_decay)
    shard_decay = jnp.exp(jnp.sum(log_decay, axis=0))
    identity = (jnp.ones((head_count,), jnp.float32), jnp.zeros_like(end_state))
    _, carry_in = entering((shard_decay, end_state), "seq", join_states, identity)
    entered = jnp.exp(jnp.dot(lower_ones(row_count), log_decay, precision=lax.Precision.HIGHEST))
    from_before = jnp.dot(
        state_read.astype(jnp.float32), carry_in, precision=lax.Precision.HIGHEST
    ) * jnp.repeat(entered, head_width, axis=1)
    mixed = local_out + from_before + jnp.repeat(skip_gain, head_width)[None, :] * wide_in
    head_table = (
        jnp.arange(width, dtype=jnp.int32)[:, None] // head_width
        == jnp.arange(head_count, dtype=jnp.int32)[None, :]
    ).astype(jnp.float32)
    square_mean = jnp.dot(mixed * mixed, head_table, precision=lax.Precision.HIGHEST) / head_width
    scale = jnp.repeat(lax.rsqrt(square_mean + 1e-05), head_width, axis=1)
    posterior = (mixed * scale * post_gain[None, :]).astype(jnp.bfloat16)
    latent = regroup_rows(posterior, start_index)
    values, final_latent = imagine(
        latent, step_noise, act_weight, dyn_weight, act_in_weight, out_weight, value_weight
    )
    return (posterior, values, final_latent)


def solution(mesh):
    placed = (
        P(("groups", "seq"), None),
        P(("groups", "seq"), None),
        P(("groups", "seq"), None),
        P(("groups", "seq"), None),
        P(),
        P(),
        P(("groups", "seq")),
        P(None, ("groups", "seq"), None),
        P(),
        P(),
        P(),
        P(),
        P(),
    )
    return jax.shard_map(
        per_device,
        mesh=mesh,
        in_specs=placed,
        out_specs=(
            P(("groups", "seq"), None),
            P(None, ("groups", "seq")),
            P(("groups", "seq"), None),
        ),
        check_vma=False,
    )
```

profile of v0, /device:TPU:0, one launch (start us, length us, event | category | flops | bytes accessed | tf_op | source)
XLA Modules:
  0.0 165.3 jit_solution(9370423981715717801)
XLA Ops:
  7.3 0.9 fusion.44
  8.2 0.2 slice_reduce_fusion
  8.7 1.3 copy.32
  10.1 2.3 %fusion.11 = f32[64,2048]{1,0:T(8,128)} fusion(bf16[128,64]{0,1:T(8,128)(2,1)} %param.16, f32[128,2048]{0,1:T(8,128)S(1)} %bitcast.98, bf16[128,2048]{0,1:T(8,128)(2,1)S(1)} %copy.32, f32[2048]{0:T(1024)S(1)} %mul.144), kind=kOutput, calls=%fused_computation.22 | convolution fusion | flops 201981952 | bytes 2121728 | tf_op jit(solution)/shard_map/while/body/eval_jaxpr/sn,sd->nd/dot_general | solution.py:58
  12.6 1.0 scatter_custom_fusion
  13.6 0.7 all_to_all.13
  14.3 7.4 %all-to-all-start = ((s32[16,1,8]{2,1,0:T(1,128)}), s32[16,1,8]{2,1,0:T(1,128)S(1)}, u32[]{:S(2)}, u32[]{:S(2)}) async-start(s32[16,1,8]{2,1,0:T(1,128)} %bitcast.12), calls=%async_computation | async-start | bytes 16384 | tf_op jit(solution)/shard_map/all_to_all | solution.py:103
  21.9 0.6 dynamic-slice.5
  23.5 2.5 %fusion.12 = f32[32,128,64]{1,2,0:T(8,128)S(1)} fusion(bf16[128,32,64]{0,2,1:T(8,128)(2,1)S(1)} %bitcast.97, f32[128,128]{1,0:T(8,128)S(1)} %fusion.53, f32[32,128]{1,0:T(8,128)S(1)} %bitcast.101, pred[128,128]{1,0:T(8,128)(4,1)S(1)} %iota_compare_fusion.2), kind=kOutput, calls=%fused_computation.23 | convolution fusion | flops 404226048 | bytes 1671168 | tf_op jit(solution)/shard_map/while/body/eval_jaxpr/hts,shp->thp/dot_general | solution.py:46
  26.0 1.6 fusion.5
  27.7 35.1 %all-reduce = f32[512]{0:T(512)S(1)} all-reduce(f32[512]{0:T(512)S(1)} %exponential_dynamic-update-slice_fusion), channel_id=2, replica_groups=mesh['groups'=2,'seq'=16] {'seq'}, use_global_device_ids=true, to_apply=%add | all-reduce | flops 512 | bytes 4096
  63.4 26.4 %all-gather.4.cloned.1.call-done = f32[1024,2048]{1,0:T(8,128)} async-done(((f32[64,2048]{1,0:T(8,128)}), f32[1024,2048]{1,0:T(8,128)}) %all-gather.4.cloned.1.call-update) | async-done | bytes 8388624 | tf_op jit(solution)/shard_map/all_gather | solution.py:9
  89.8 26.5 %while.9 = (s32[]{:T(128)}, f32[64,2048]{1,0:T(8,128)S(1)}, s32[]{:T(128)}, f32[16,32]{1,0:T(8,128)S(1)}, f32[16,64,2048]{2,1,0:T(8,128)}, /*index=5*/s32[]{:T(128)}, s32[]{:T(128)}) while((s32[]{:T(128)}, f32[64,2048]{1,0:T(8,128)S(1)}, s32[]{:T(128)}, f32[16,32]{1,0:T(8,128)S(1)}, f32[16,64,2048]{2,1,0:T(8,128)}, ...), condition=%wide.region_2.3_spmd.clone, body=%wide.region_1.2_spmd.clone.sunk | while | flops 524292 | bytes 1606121 | solution.py:21
  89.9 1.5 fusion.87
  91.6 1.5 fusion.87
  93.2 1.5 fusion.87
  94.9 1.5 fusion.87
  96.5 1.5 fusion.87
  98.2 1.5 fusion.87
  99.9 1.5 fusion.87
  101.5 1.5 fusion.87
  103.2 1.5 fusion.87
  104.8 1.5 fusion.87
  106.5 1.5 fusion.87
  108.1 1.5 fusion.87
  109.8 1.5 fusion.87
  111.5 1.5 fusion.87
  113.1 1.5 fusion.87
  114.8 1.5 fusion.87
  116.3 2.5 %fusion.3 = f32[128,2048]{0,1:T(8,128)S(1)} fusion(f32[128,2048]{0,1:T(8,128)} %fusion.5, f32[128,2048]{0,1:T(8,128)S(1)} %bitcast.96, f32[64,2048]{1,0:T(8,128)S(1)} %get-tuple-element.124, bf16[128,64]{0,1:T(8,128)(2,1)S(1)} %copy-done.8, bf16[128,2048]{0,1:T(8,128)(2,1)S(1)} %copy.32, f32[2048]{0:T(1024)S(1)} %mul.148), kind=kOutput, calls=%fused_computation.12 | convolution fusion | flops 202637312 | bytes 4218880 | tf_op jit(solution)/shard_map/dot_general | solution.py:156
  118.8 1.3 fusion.24
  120.1 0.3 fusion.29
  120.7 0.9 gather_fusion
  121.7 0.9 bitcast_select_fusion
  122.6 3.8 %all-to-all-start.1 = ((bf16[16,8,2048]{2,1,0:T(8,128)(2,1)}), bf16[16,8,2048]{2,1,0:T(8,128)(2,1)S(1)}, u32[]{:S(2)}, u32[]{:S(2)}) async-start(bf16[16,8,2048]{2,1,0:T(8,128)(2,1)} %bitcast_select_fusion), calls=%async_computation.1 | async-start | bytes 1048576 | tf_op jit(solution)/shard_map/all_to_all | solution.py:105
  126.4 14.0 %all-to-all-done.1 = bf16[16,8,2048]{2,1,0:T(8,128)(2,1)S(1)} async-done(((bf16[16,8,2048]{2,1,0:T(8,128)(2,1)}), bf16[16,8,2048]{2,1,0:T(8,128)(2,1)S(1)}, u32[]{:S(2)}, u32[]{:S(2)}) %all-to-all-start.1) | async-done | bytes 524320 | tf_op jit(solution)/shard_map/all_to_all | solution.py:105
  140.4 0.9 gather_fusion.1
  141.3 0.3 fusion.26
  141.7 0.5 fusion.22
  142.2 3.3 %fusion.38 = bf16[128,1024]{1,0:T(8,128)(2,1)S(1)} fusion(f32[128,1024]{1,0:T(8,128)S(1)} %fusion.22, bf16[2048,1024]{1,0:T(8,128)(2,1)} %param.24, bf16[3,128,1024]{2,1,0:T(8,128)(2,1)} %param.22, f32[128]{0:T(128)S(1)} %add_rsqrt_fusion.2, bf16[128,2048]{1,0:T(8,128)(2,1)S(1)} %gather_fusion.1, pred[128]{0:T(512)(128)(4,1)S(1)} %get-tuple-element.162), kind=kOutput, calls=%fused_computation.70 | convolution fusion | flops 538968064 | bytes 5767808 | tf_op jit(solution)/shard_map/dot_general | solution.py:119
  145.7 1.0 multiply_reduce_fusion.1
  146.7 0.5 fusion.21
  147.2 3.3 %fusion.37 = bf16[128,1024]{1,0:T(8,128)(2,1)S(1)} fusion(f32[128,1024]{1,0:T(8,128)S(1)} %fusion.21, bf16[2048,1024]{1,0:T(8,128)(2,1)} %param.24, bf16[3,128,1024]{2,1,0:T(8,128)(2,1)} %param.22, f32[128,2048]{1,0:T(8,128)S(1)} %get-tuple-element.169, f32[128]{0:T(128)S(1)} %add_rsqrt_fusion.1), kind=kOutput, calls=%fused_computation.68 | convolution fusion | flops 538443776 | bytes 6291968 | tf_op jit(solution)/shard_map/dot_general | solution.py:119
  150.8 0.9 multiply_reduce_fusion
  151.7 0.5 fusion.20
  152.2 3.3 %fusion.36 = bf16[128,1024]{1,0:T(8,128)(2,1)S(1)} fusion(f32[128,1024]{1,0:T(8,128)S(1)} %fusion.20, bf16[2048,1024]{1,0:T(8,128)(2,1)} %param.24, bf16[3,128,1024]{2,1,0:T(8,128)(2,1)} %param.22, f32[128,2048]{1,0:T(8,128)S(1)} %get-tuple-element.171, f32[128]{0:T(128)S(1)} %add_rsqrt_fusion), kind=kOutput, calls=%fused_computation.66 | convolution fusion | flops 538443776 | bytes 6291968 | tf_op jit(solution)/shard_map/dot_general | solution.py:119
  155.8 1.6 fusion.10
  157.9 0.6 pad_maximum_fusion
  (118 shorter events, 5.5 us)
Async XLA Ops:
  7.2 134.5 %copy-start = (bf16[2048,128]{1,0:T(8,128)(2,1)S(1)}, bf16[2048,128]{1,0:T(8,128)(2,1)}, u32[]{:S(2)}) copy-start(bf16[2048,128]{1,0:T(8,128)(2,1)} %param.23) | copy-start | bytes 1572868
  7.2 14.7 %copy-start.15 = (u32[32]{0:T(128)S(1)}, u32[32]{0:T(128)}, u32[]{:S(2)}) copy-start(u32[32]{0:T(128)} %constant.141) | copy-start | bytes 388
  7.2 14.5 %copy-start.10 = (f32[128,32]{0,1:T(8,128)S(1)}, f32[128,32]{0,1:T(8,128)}, u32[]{:S(2)}) copy-start(f32[128,32]{0,1:T(8,128)} %param.18) | copy-start | bytes 49156
  7.2 16.1 %copy-start.9 = (bf16[128,64]{0,1:T(8,128)(2,1)S(1)}, bf16[128,64]{0,1:T(8,128)(2,1)}, u32[]{:S(2)}) copy-start(bf16[128,64]{0,1:T(8,128)(2,1)} %param.16) | copy-start | bytes 49156
  7.2 5.2 %copy-start.14 = (s32[128]{0:T(128)S(1)}, s32[128]{0:T(128)}, u32[]{:S(2)}) copy-start(s32[128]{0:T(128)} %param.21) | copy-start | bytes 1540
  7.2 16.0 %copy-start.8 = (bf16[128,64]{0,1:T(8,128)(2,1)S(1)}, bf16[128,64]{0,1:T(8,128)(2,1)}, u32[]{:S(2)}) copy-start(bf16[128,64]{0,1:T(8,128)(2,1)} %param.17) | copy-start | bytes 49156
  7.2 82.5 %all-gather.4.cloned.1.call-start = ((), (), s32[]{:S(2)}) async-start(), calls=%async_computation.2 | async-start | bytes 8912896 | tf_op jit(solution)/shard_map/all_gather | solution.py:9
  12.4 50.5 %copy-start.13 = (f32[32]{0:T(128)S(1)}, f32[32]{0:T(128)}, u32[]{:S(2)}) copy-start(f32[32]{0:T(128)} %param.19) | copy-start | bytes 388
  14.3 48.7 %all-to-all-start = ((s32[16,1,8]{2,1,0:T(1,128)}), s32[16,1,8]{2,1,0:T(1,128)S(1)}, u32[]{:S(2)}, u32[]{:S(2)}) async-start(s32[16,1,8]{2,1,0:T(1,128)} %bitcast.12), calls=%async_computation | async-start | bytes 16384 | tf_op jit(solution)/shard_map/all_to_all | solution.py:103
  116.3 3.8 %copy-start.11 = (f32[2048]{0:T(1024)S(1)}, f32[2048]{0:T(1024)}, u32[]{:S(2)}) copy-start(f32[2048]{0:T(1024)} %param.20) | copy-start | bytes 24580
  120.5 5.9 %copy-start.12 = (bf16[1024]{0:T(1024)(128)(2,1)S(1)}, bf16[1024]{0:T(1024)(128)(2,1)}, u32[]{:S(2)}) copy-start(bf16[1024]{0:T(1024)(128)(2,1)} %param.27) | copy-start | bytes 6148
  120.7 20.6 %copy-start.1 = (bf16[128,2048]{1,0:T(8,128)(2,1)}, bf16[128,2048]{1,0:T(8,128)(2,1)S(1)}, u32[]{:S(2)}) copy-start(bf16[128,2048]{1,0:T(8,128)(2,1)S(1)} %copy.40) | copy-start | bytes 1572868
  121.6 20.0 %copy-start.5 = (bf16[128,1024]{1,0:T(8,128)(2,1)S(1)}, bf16[128,1024]{1,0:T(8,128)(2,1)}, u32[]{:S(2)}) copy-start(bf16[128,1024]{1,0:T(8,128)(2,1)} %param.25) | copy-start | bytes 786436
  122.6 17.8 %all-to-all-start.1 = ((bf16[16,8,2048]{2,1,0:T(8,128)(2,1)}), bf16[16,8,2048]{2,1,0:T(8,128)(2,1)S(1)}, u32[]{:S(2)}, u32[]{:S(2)}) async-start(bf16[16,8,2048]{2,1,0:T(8,128)(2,1)} %bitcast_select_fusion), calls=%async_computation.1 | async-start | bytes 1048576 | tf_op jit(solution)/shard_map/all_to_all | solution.py:105
  142.2 3.5 %copy-start.2 = (bf16[1024,2048]{1,0:T(8,128)(2,1)S(1)}, bf16[1024,2048]{1,0:T(8,128)(2,1)}, u32[]{:S(2)}) copy-start(bf16[1024,2048]{1,0:T(8,128)(2,1)} %param.26) | copy-start | bytes 12582916
  147.2 3.5 %copy-start.3 = (bf16[1024,2048]{1,0:T(8,128)(2,1)S(1)}, bf16[1024,2048]{1,0:T(8,128)(2,1)}, u32[]{:S(2)}) copy-start(bf16[1024,2048]{1,0:T(8,128)(2,1)} %param.26) | copy-start | bytes 12582916
  150.8 0.9 copy-start.6
  152.2 3.5 %copy-start.4 = (bf16[1024,2048]{1,0:T(8,128)(2,1)S(1)}, bf16[1024,2048]{1,0:T(8,128)(2,1)}, u32[]{:S(2)}) copy-start(bf16[1024,2048]{1,0:T(8,128)(2,1)} %param.26) | copy-start | bytes 12582916
  155.8 1.7 %copy-start.7 = (bf16[128,1024]{1,0:T(8,128)(2,1)S(1)}, bf16[128,1024]{1,0:T(8,128)(2,1)}, u32[]{:S(2)}) copy-start(bf16[128,1024]{1,0:T(8,128)(2,1)} %copy-done.6) | copy-start | bytes 786436
Sparse Core Ops, SparseCore 0:
  12.5 77.1 all-gather.3
where the time goes:
time: 167 us; the launch traced here: 165 us
  waiting for transfers between devices  40.4 us (24%)
  blocking collectives  35.1 us (21%)
  matrix products  27 us (16%)
  other arithmetic  26.2 us (16%)
  between operations  15.1 us (9%)
  starting transfers between devices  11.2 us (7%)
  local copies, waits for them, and re-layouts  9.99 us (6%)
    unnamed x1, blocking collectives  35.1 us
    all_gather x1, waiting for transfers between devices, entering(): everything = jax.tree.map(lambda part: lax.all_gather(part, axis), shard)  26.4 us
    select_n x16, other arithmetic, lap(): return jax.tree.map(lambda a, b: jnp.where(reached, a, b), new, before)  23.7 us
    all_to_all x1, waiting for transfers between devices, regroup_rows(): lax.all_to_all(picked, 'seq', split_axis=0, concat_axis=0, tiled=True)  14 us
    dot_general x3, matrix products, imagine(): jnp.dot(normed, dyn_weight, preferred_element_type=jnp.float32)  9.93 us
    all_to_all x1, starting transfers between devices, regroup_rows(): lax.all_to_all(wanted, 'seq', split_axis=0, concat_axis=0, tiled=True)  7.41 us
    all_to_all x1, starting transfers between devices, regroup_rows(): lax.all_to_all(picked, 'seq', split_axis=0, concat_axis=0, tiled=True)  3.75 us
    dot_general x3, matrix products, imagine(): jnp.dot(hidden, out_weight, preferred_element_type=jnp.float32)  3.44 us
  transfers between devices with their start and end apart: 3, of which 2 were waited for; matrix products, arithmetic and copies ran while one was open for 4% of the time, Pallas kernels for 0%

commit v1 on v0

--- a/solution.py
+++ b/solution.py
@@ -2,6 +2,30 @@
 import jax.numpy as jnp
 from jax import lax
 from jax.sharding import PartitionSpec as P
+
+
+def split_up(shard, dim, size):
+    dims = shard.shape
+    pieces = shard.reshape(*dims[:dim], size, dims[dim] // size, *dims[dim + 1 :])
+    return jnp.moveaxis(pieces, dim, 0)
+
+
+def laid_out(pieces, dim):
+    pieces = jnp.moveaxis(pieces, 0, dim)
+    lengths = pieces.shape
+    return pieces.reshape(*lengths[:dim], lengths[dim] * lengths[dim + 1], *lengths[dim + 2 :])
+
+
+def sent_to_each(value, axis, split_dim, concat_dim):
+    size, mine = (lax.axis_size(axis), lax.axis_index(axis))
+    tiles = split_up(value, split_dim, size)
+    whole = tiles
+    for turn in range(1, size):
+        target, source = ((mine + turn) % size, (mine - turn) % size)
+        sent = lax.dynamic_index_in_dim(tiles, target, 0)
+        received = lax.ppermute(sent, axis, [(i, (i + turn) % size) for i in range(size)])
+        whole = lax.dynamic_update_slice_in_dim(whole, received, source, axis=0)
+    return laid_out(whole, concat_dim)
 
 
 def entering(shard, axis, combine, identity):
@@ -102,7 +126,7 @@
     picked = jnp.take(
         posterior, lax.all_to_all(wanted, "seq", split_axis=0, concat_axis=0, tiled=True), axis=0
     )
-    landed = lax.all_to_all(picked, "seq", split_axis=0, concat_axis=0, tiled=True)
+    landed = sent_to_each(picked, "seq", 0, 0)
     return jnp.take(landed.reshape(peer_count * slot_cap, posterior.shape[1]), slot_index, axis=0)
 
 

time: 167 us -> 172 us (1.030)
  starting transfers between devices: 11.2 us -> 28.1 us
  waiting for transfers between devices: 40.4 us -> 29.5 us
    ppermute x0 -> x15, starting transfers between devices: none -> 20.6 us  [sent_to_each(): lax.ppermute(sent, axis, [(i, (i + turn) % size) for i in range(size)])]
    all_to_all x1 -> x0, waiting for transfers between devices: 14 us -> none  [regroup_rows(): lax.all_to_all(picked, 'seq', split_axis=0, concat_axis=0, tiled=True)]
    all_to_all x1 -> x0, starting transfers between devices: 3.75 us -> none  [regroup_rows(): lax.all_to_all(picked, 'seq', split_axis=0, concat_axis=0, tiled=True)]
    ppermute x0 -> x15, waiting for transfers between devices: none -> 3.51 us  [sent_to_each(): lax.ppermute(sent, axis, [(i, (i + turn) % size) for i in range(size)])]
  transfers between devices with their start and end apart: 3 -> 17, of which waited for: 2 -> 4; matrix products, arithmetic and copies ran while one was open for 4% -> 4% of each run, Pallas kernels for 0% -> 0%
where the time goes in v1:
time: 172 us; the launch traced here: 171 us
  blocking collectives  35.1 us (20%)
  waiting for transfers between devices  29.5 us (17%)
  starting transfers between devices  28.1 us (16%)
  matrix products  27 us (16%)
  other arithmetic  25.5 us (15%)
  between operations  15.7 us (9%)
  local copies, waits for them, and re-layouts  10.2 us (6%)
    unnamed x1, blocking collectives  35.1 us
    all_gather x1, waiting for transfers between devices, entering(): everything = jax.tree.map(lambda part: lax.all_gather(part, axis), shard)  25.9 us
    select_n x16, other arithmetic, lap(): return jax.tree.map(lambda a, b: jnp.where(reached, a, b), new, before)  23.7 us
    ppermute x15, starting transfers between devices, sent_to_each(): lax.ppermute(sent, axis, [(i, (i + turn) % size) for i in range(size)])  20.6 us
    dot_general x3, matrix products, imagine(): jnp.dot(normed, dyn_weight, preferred_element_type=jnp.float32)  9.93 us
    all_to_all x1, starting transfers between devices, regroup_rows(): lax.all_to_all(wanted, 'seq', split_axis=0, concat_axis=0, tiled=True)  7.41 us
    ppermute x15, waiting for transfers between devices, sent_to_each(): lax.ppermute(sent, axis, [(i, (i + turn) % size) for i in range(size)])  3.51 us
  transfers between devices with their start and end apart: 17, of which 4 were waited for; matrix products, arithmetic and copies ran while one was open for 4% of the time, Pallas kernels for 0%

profile of v1, /device:TPU:0, one launch (start us, length us, event | category | flops | bytes accessed | tf_op | source)
XLA Modules:
  0.0 171.3 jit_solution(8304268656404585611)
XLA Ops:
  7.3 0.9 fusion.44
  8.7 1.3 copy.34
  10.1 2.3 %fusion.11 = f32[64,2048]{1,0:T(8,128)} fusion(bf16[128,64]{0,1:T(8,128)(2,1)} %param.16, f32[128,2048]{0,1:T(8,128)S(1)} %bitcast.130, bf16[128,2048]{0,1:T(8,128)(2,1)S(1)} %copy.34, f32[2048]{0:T(1024)S(1)} %mul.144), kind=kOutput, calls=%fused_computation.22 | convolution fusion | flops 201981952 | bytes 2121728 | tf_op jit(solution)/shard_map/while/body/eval_jaxpr/sn,sd->nd/dot_general | solution.py:82
  12.6 1.0 scatter_custom_fusion
  14.3 7.4 %all-to-all-start = ((s32[16,1,8]{2,1,0:T(1,128)}), s32[16,1,8]{2,1,0:T(1,128)S(1)}, u32[]{:S(2)}, u32[]{:S(2)}) async-start(s32[16,1,8]{2,1,0:T(1,128)} %bitcast.12), calls=%async_computation | async-start | bytes 16384 | tf_op jit(solution)/shard_map/all_to_all | solution.py:127
  23.8 35.1 %all-reduce = f32[512]{0:T(512)S(1)} all-reduce(f32[512]{0:T(512)S(1)} %exponential_dynamic-update-slice_fusion), channel_id=2, replica_groups=mesh['groups'=2,'seq'=16] {'seq'}, use_global_device_ids=true, to_apply=%add | all-reduce | flops 512 | bytes 4096
  59.4 2.5 %fusion.12 = f32[32,128,64]{1,2,0:T(8,128)S(1)} fusion(bf16[128,32,64]{0,2,1:T(8,128)(2,1)S(1)} %bitcast.129, f32[128,128]{1,0:T(8,128)S(1)} %fusion.53, f32[32,128]{1,0:T(8,128)S(1)} %bitcast.133, pred[128,128]{1,0:T(8,128)(4,1)S(1)} %iota_compare_fusion.2), kind=kOutput, calls=%fused_computation.23 | convolution fusion | flops 404226048 | bytes 1671168 | tf_op jit(solution)/shard_map/while/body/eval_jaxpr/hts,shp->thp/dot_general | solution.py:70
  62.0 1.6 fusion.5
  63.9 25.9 %all-gather.4.cloned.1.call-done = f32[1024,2048]{1,0:T(8,128)} async-done(((f32[64,2048]{1,0:T(8,128)}), f32[1024,2048]{1,0:T(8,128)}) %all-gather.4.cloned.1.call-update) | async-done | bytes 8388624 | tf_op jit(solution)/shard_map/all_gather | solution.py:33
  89.9 26.5 %while.9 = (s32[]{:T(128)}, f32[64,2048]{1,0:T(8,128)S(1)}, s32[]{:T(128)}, f32[16,32]{1,0:T(8,128)S(1)}, f32[16,64,2048]{2,1,0:T(8,128)}, /*index=5*/s32[]{:T(128)}, s32[]{:T(128)}) while((s32[]{:T(128)}, f32[64,2048]{1,0:T(8,128)S(1)}, s32[]{:T(128)}, f32[16,32]{1,0:T(8,128)S(1)}, f32[16,64,2048]{2,1,0:T(8,128)}, ...), condition=%wide.region_2.3_spmd.clone, body=%wide.region_1.2_spmd.clone.sunk | while | flops 524292 | bytes 1606121 | solution.py:45
  90.0 1.5 fusion.87
  91.7 1.5 fusion.87
  93.3 1.5 fusion.87
  95.0 1.5 fusion.87
  96.7 1.5 fusion.87
  98.3 1.5 fusion.87
  100.0 1.5 fusion.87
  101.6 1.5 fusion.87
  103.3 1.5 fusion.87
  105.0 1.5 fusion.87
  106.6 1.5 fusion.87
  108.3 1.5 fusion.87
  109.9 1.5 fusion.87
  111.6 1.5 fusion.87
  113.2 1.5 fusion.87
  114.9 1.5 fusion.87
  116.4 2.5 %fusion.3 = f32[128,2048]{0,1:T(8,128)S(1)} fusion(f32[128,2048]{0,1:T(8,128)} %fusion.5, f32[128,2048]{0,1:T(8,128)S(1)} %bitcast.128, f32[64,2048]{1,0:T(8,128)S(1)} %get-tuple-element.124, bf16[128,64]{0,1:T(8,128)(2,1)S(1)} %copy-done.8, bf16[128,2048]{0,1:T(8,128)(2,1)S(1)} %copy.34, f32[2048]{0:T(1024)S(1)} %mul.148), kind=kOutput, calls=%fused_computation.12 | convolution fusion | flops 202637312 | bytes 4218880 | tf_op jit(solution)/shard_map/dot_general | solution.py:180
  118.9 1.3 fusion.24
  120.8 0.9 gather_fusion
  123.0 2.0 %collective-permute-start.2 = (bf16[1,1,8,2048]{3,2,0,1:T(8,128)(2,1)S(1)}, bf16[1,1,8,2048]{3,2,0,1:T(8,128)(2,1)S(1)}, u32[]{:S(2)}, u32[]{:S(2)}) collective-permute-start(bf16[1,1,8,2048]{3,2,0,1:T(8,128)(2,1)S(1)} %get-tuple-element.176), channel_id=1, source_target_pairs={{0,3},{1,4},{2,5},{3,6},{4,7},{5,8},{6,9},{7,10},{8,11},{9,12},{10... | collective-permute-start | bytes 98312 | tf_op jit(solution)/shard_map/ppermute | solution.py:26
  125.0 1.2 collective-permute-start.3
  126.2 1.9 %collective-permute-done = bf16[1,1,8,2048]{3,2,0,1:T(8,128)(2,1)S(1)} collective-permute-done((bf16[1,1,8,2048]{3,2,0,1:T(8,128)(2,1)S(1)}, bf16[1,1,8,2048]{3,2,0,1:T(8,128)(2,1)S(1)}, u32[]{:S(2)}, u32[]{:S(2)}) %collective-permute-start) | collective-permute-done | bytes 32800 | tf_op jit(solution)/shard_map/ppermute | solution.py:26
  128.1 0.9 collective-permute-start.5
  129.1 2.7 %collective-permute-start.6 = (bf16[1,1,8,2048]{3,2,0,1:T(8,128)(2,1)S(1)}, bf16[1,1,8,2048]{3,2,0,1:T(8,128)(2,1)S(1)}, u32[]{:S(2)}, u32[]{:S(2)}) collective-permute-start(bf16[1,1,8,2048]{3,2,0,1:T(8,128)(2,1)S(1)} %get-tuple-element.172), channel_id=1, source_target_pairs={{0,7},{1,8},{2,9},{3,10},{4,11},{5,12},{6,13},{7,14},{8,15},{9,0},... | collective-permute-start | bytes 98312 | tf_op jit(solution)/shard_map/ppermute | solution.py:26
  131.8 1.8 %collective-permute-start.7 = (bf16[1,1,8,2048]{3,2,0,1:T(8,128)(2,1)S(1)}, bf16[1,1,8,2048]{3,2,0,1:T(8,128)(2,1)S(1)}, u32[]{:S(2)}, u32[]{:S(2)}) collective-permute-start(bf16[1,1,8,2048]{3,2,0,1:T(8,128)(2,1)S(1)} %get-tuple-element.171), channel_id=1, source_target_pairs={{0,8},{1,9},{2,10},{3,11},{4,12},{5,13},{6,14},{7,15},{8,0},{9,1},... | collective-permute-start | bytes 98312 | tf_op jit(solution)/shard_map/ppermute | solution.py:26
  133.7 1.5 collective-permute-start.9
  135.2 3.6 %collective-permute-start.10 = (bf16[1,1,8,2048]{3,2,0,1:T(8,128)(2,1)S(1)}, bf16[1,1,8,2048]{3,2,0,1:T(8,128)(2,1)S(1)}, u32[]{:S(2)}, u32[]{:S(2)}) collective-permute-start(bf16[1,1,8,2048]{3,2,0,1:T(8,128)(2,1)S(1)} %get-tuple-element.168), channel_id=1, source_target_pairs={{0,11},{1,12},{2,13},{3,14},{4,15},{5,0},{6,1},{7,2},{8,3},{9,4},{... | collective-permute-start | bytes 98312 | tf_op jit(solution)/shard_map/ppermute | solution.py:26
  138.7 0.7 collective-permute-start.11
  140.1 2.0 %collective-permute-start.13 = (bf16[1,1,8,2048]{3,2,0,1:T(8,128)(2,1)S(1)}, bf16[1,1,8,2048]{3,2,0,1:T(8,128)(2,1)S(1)}, u32[]{:S(2)}, u32[]{:S(2)}) collective-permute-start(bf16[1,1,8,2048]{3,2,0,1:T(8,128)(2,1)S(1)} %get-tuple-element.165), channel_id=1, source_target_pairs={{0,14},{1,15},{2,0},{3,1},{4,2},{5,3},{6,4},{7,5},{8,6},{9,7},{10,... | collective-permute-start | bytes 98312 | tf_op jit(solution)/shard_map/ppermute | solution.py:26
  142.1 2.7 %collective-permute-start.14 = (bf16[1,1,8,2048]{3,2,0,1:T(8,128)(2,1)S(1)}, bf16[1,1,8,2048]{3,2,0,1:T(8,128)(2,1)S(1)}, u32[]{:S(2)}, u32[]{:S(2)}) collective-permute-start(bf16[1,1,8,2048]{3,2,0,1:T(8,128)(2,1)S(1)} %get-tuple-element.164), channel_id=1, source_target_pairs={{0,15},{1,0},{2,1},{3,2},{4,3},{5,4},{6,5},{7,6},{8,7},{9,8},{10,9... | collective-permute-start | bytes 98312 | tf_op jit(solution)/shard_map/ppermute | solution.py:26
  144.9 1.5 collective-permute-done.14
  146.4 0.9 gather_fusion.1
  148.2 3.3 %fusion.38 = bf16[128,1024]{1,0:T(8,128)(2,1)S(1)} fusion(f32[128,1024]{1,0:T(8,128)S(1)} %fusion.22, bf16[2048,1024]{1,0:T(8,128)(2,1)} %param.24, bf16[3,128,1024]{2,1,0:T(8,128)(2,1)} %param.22, f32[128]{0:T(128)S(1)} %add_rsqrt_fusion.2, bf16[128,2048]{1,0:T(8,128)(2,1)S(1)} %gather_fusion.1, pred[128]{0:T(512)(128)(4,1)S(1)} %get-tuple-element.162), kind=kOutput, calls=%fused_computation.70 | convolution fusion | flops 538968064 | bytes 5767808 | tf_op jit(solution)/shard_map/dot_general | solution.py:143
  151.7 1.0 multiply_reduce_fusion.1
  153.3 3.3 %fusion.37 = bf16[128,1024]{1,0:T(8,128)(2,1)S(1)} fusion(f32[128,1024]{1,0:T(8,128)S(1)} %fusion.21, bf16[2048,1024]{1,0:T(8,128)(2,1)} %param.24, bf16[3,128,1024]{2,1,0:T(8,128)(2,1)} %param.22, f32[128,2048]{1,0:T(8,128)S(1)} %get-tuple-element.184, f32[128]{0:T(128)S(1)} %add_rsqrt_fusion.1), kind=kOutput, calls=%fused_computation.68 | convolution fusion | flops 538443776 | bytes 6291968 | tf_op jit(solution)/shard_map/dot_general | solution.py:143
  156.8 0.9 multiply_reduce_fusion
  158.2 3.3 %fusion.36 = bf16[128,1024]{1,0:T(8,128)(2,1)S(1)} fusion(f32[128,1024]{1,0:T(8,128)S(1)} %fusion.20, bf16[2048,1024]{1,0:T(8,128)(2,1)} %param.24, bf16[3,128,1024]{2,1,0:T(8,128)(2,1)} %param.22, f32[128,2048]{1,0:T(8,128)S(1)} %get-tuple-element.186, f32[128]{0:T(128)S(1)} %add_rsqrt_fusion), kind=kOutput, calls=%fused_computation.66 | convolution fusion | flops 538443776 | bytes 6291968 | tf_op jit(solution)/shard_map/dot_general | solution.py:143
  161.8 1.6 fusion.10
  (163 shorter events, 12.0 us)
Async XLA Ops:
  7.2 140.5 %copy-start = (bf16[2048,128]{1,0:T(8,128)(2,1)S(1)}, bf16[2048,128]{1,0:T(8,128)(2,1)}, u32[]{:S(2)}) copy-start(bf16[2048,128]{1,0:T(8,128)(2,1)} %param.23) | copy-start | bytes 1572868
  7.2 15.2 %copy-start.15 = (u32[32]{0:T(128)S(1)}, u32[32]{0:T(128)}, u32[]{:S(2)}) copy-start(u32[32]{0:T(128)} %constant.355) | copy-start | bytes 388
  7.2 15.0 %copy-start.10 = (f32[128,32]{0,1:T(8,128)S(1)}, f32[128,32]{0,1:T(8,128)}, u32[]{:S(2)}) copy-start(f32[128,32]{0,1:T(8,128)} %param.18) | copy-start | bytes 49156
  7.2 52.0 %copy-start.9 = (bf16[128,64]{0,1:T(8,128)(2,1)S(1)}, bf16[128,64]{0,1:T(8,128)(2,1)}, u32[]{:S(2)}) copy-start(bf16[128,64]{0,1:T(8,128)(2,1)} %param.16) | copy-start | bytes 49156
  7.2 5.2 %copy-start.14 = (s32[128]{0:T(128)S(1)}, s32[128]{0:T(128)}, u32[]{:S(2)}) copy-start(s32[128]{0:T(128)} %param.21) | copy-start | bytes 1540
  7.2 51.7 %copy-start.13 = (f32[32]{0:T(128)S(1)}, f32[32]{0:T(128)}, u32[]{:S(2)}) copy-start(f32[32]{0:T(128)} %param.19) | copy-start | bytes 388
  7.2 51.8 %copy-start.12 = (bf16[1024]{0:T(1024)(128)(2,1)S(1)}, bf16[1024]{0:T(1024)(128)(2,1)}, u32[]{:S(2)}) copy-start(bf16[1024]{0:T(1024)(128)(2,1)} %param.27) | copy-start | bytes 6148
  7.2 51.9 %copy-start.8 = (bf16[128,64]{0,1:T(8,128)(2,1)S(1)}, bf16[128,64]{0,1:T(8,128)(2,1)}, u32[]{:S(2)}) copy-start(bf16[128,64]{0,1:T(8,128)(2,1)} %param.17) | copy-start | bytes 49156
  7.3 82.6 %all-gather.4.cloned.1.call-start = ((), (), s32[]{:S(2)}) async-start(), calls=%async_computation.1 | async-start | bytes 8912896 | tf_op jit(solution)/shard_map/all_gather | solution.py:33
  14.3 49.3 %all-to-all-start = ((s32[16,1,8]{2,1,0:T(1,128)}), s32[16,1,8]{2,1,0:T(1,128)S(1)}, u32[]{:S(2)}, u32[]{:S(2)}) async-start(s32[16,1,8]{2,1,0:T(1,128)} %bitcast.12), calls=%async_computation | async-start | bytes 16384 | tf_op jit(solution)/shard_map/all_to_all | solution.py:127
  116.4 3.8 %copy-start.11 = (f32[2048]{0:T(1024)S(1)}, f32[2048]{0:T(1024)}, u32[]{:S(2)}) copy-start(f32[2048]{0:T(1024)} %param.20) | copy-start | bytes 24580
  120.8 21.3 %copy-start.1 = (bf16[128,2048]{1,0:T(8,128)(2,1)}, bf16[128,2048]{1,0:T(8,128)(2,1)S(1)}, u32[]{:S(2)}) copy-start(bf16[128,2048]{1,0:T(8,128)(2,1)S(1)} %copy.43) | copy-start | bytes 1572868
  121.9 25.8 %copy-start.5 = (bf16[128,1024]{1,0:T(8,128)(2,1)S(1)}, bf16[128,1024]{1,0:T(8,128)(2,1)}, u32[]{:S(2)}) copy-start(bf16[128,1024]{1,0:T(8,128)(2,1)} %param.25) | copy-start | bytes 786436
  122.0 6.1 %collective-permute-start = (bf16[1,1,8,2048]{3,2,0,1:T(8,128)(2,1)S(1)}, bf16[1,1,8,2048]{3,2,0,1:T(8,128)(2,1)S(1)}, u32[]{:S(2)}, u32[]{:S(2)}) collective-permute-start(bf16[1,1,8,2048]{3,2,0,1:T(8,128)(2,1)S(1)} %get-tuple-element.178), channel_id=1, source_target_pairs={{0,1},{1,2},{2,3},{3,4},{4,5},{5,6},{6,7},{7,8},{8,9},{9,10},{10,1... | collective-permute-start | bytes 98312 | tf_op jit(solution)/shard_map/ppermute | solution.py:26
  122.4 6.7 %collective-permute-start.1 = (bf16[1,1,8,2048]{3,2,0,1:T(8,128)(2,1)S(1)}, bf16[1,1,8,2048]{3,2,0,1:T(8,128)(2,1)S(1)}, u32[]{:S(2)}, u32[]{:S(2)}) collective-permute-start(bf16[1,1,8,2048]{3,2,0,1:T(8,128)(2,1)S(1)} %get-tuple-element.177), channel_id=1, source_target_pairs={{0,2},{1,3},{2,4},{3,5},{4,6},{5,7},{6,8},{7,9},{8,10},{9,11},{10,... | collective-permute-start | bytes 98312 | tf_op jit(solution)/shard_map/ppermute | solution.py:26
  123.0 8.7 %collective-permute-start.2 = (bf16[1,1,8,2048]{3,2,0,1:T(8,128)(2,1)S(1)}, bf16[1,1,8,2048]{3,2,0,1:T(8,128)(2,1)S(1)}, u32[]{:S(2)}, u32[]{:S(2)}) collective-permute-start(bf16[1,1,8,2048]{3,2,0,1:T(8,128)(2,1)S(1)} %get-tuple-element.176), channel_id=1, source_target_pairs={{0,3},{1,4},{2,5},{3,6},{4,7},{5,8},{6,9},{7,10},{8,11},{9,12},{10... | collective-permute-start | bytes 98312 | tf_op jit(solution)/shard_map/ppermute | solution.py:26
  125.0 8.6 %collective-permute-start.3 = (bf16[1,1,8,2048]{3,2,0,1:T(8,128)(2,1)S(1)}, bf16[1,1,8,2048]{3,2,0,1:T(8,128)(2,1)S(1)}, u32[]{:S(2)}, u32[]{:S(2)}) collective-permute-start(bf16[1,1,8,2048]{3,2,0,1:T(8,128)(2,1)S(1)} %get-tuple-element.175), channel_id=1, source_target_pairs={{0,4},{1,5},{2,6},{3,7},{4,8},{5,9},{6,10},{7,11},{8,12},{9,13},{1... | collective-permute-start | bytes 98312 | tf_op jit(solution)/shard_map/ppermute | solution.py:26
  126.2 7.5 %collective-permute-start.4 = (bf16[1,1,8,2048]{3,2,0,1:T(8,128)(2,1)S(1)}, bf16[1,1,8,2048]{3,2,0,1:T(8,128)(2,1)S(1)}, u32[]{:S(2)}, u32[]{:S(2)}) collective-permute-start(bf16[1,1,8,2048]{3,2,0,1:T(8,128)(2,1)S(1)} %get-tuple-element.174), channel_id=1, source_target_pairs={{0,5},{1,6},{2,7},{3,8},{4,9},{5,10},{6,11},{7,12},{8,13},{9,14},{... | collective-permute-start | bytes 98312 | tf_op jit(solution)/shard_map/ppermute | solution.py:26
  128.1 7.1 %collective-permute-start.5 = (bf16[1,1,8,2048]{3,2,0,1:T(8,128)(2,1)S(1)}, bf16[1,1,8,2048]{3,2,0,1:T(8,128)(2,1)S(1)}, u32[]{:S(2)}, u32[]{:S(2)}) collective-permute-start(bf16[1,1,8,2048]{3,2,0,1:T(8,128)(2,1)S(1)} %get-tuple-element.173), channel_id=1, source_target_pairs={{0,6},{1,7},{2,8},{3,9},{4,10},{5,11},{6,12},{7,13},{8,14},{9,15},... | collective-permute-start | bytes 98312 | tf_op jit(solution)/shard_map/ppermute | solution.py:26
  129.1 9.7 %collective-permute-start.6 = (bf16[1,1,8,2048]{3,2,0,1:T(8,128)(2,1)S(1)}, bf16[1,1,8,2048]{3,2,0,1:T(8,128)(2,1)S(1)}, u32[]{:S(2)}, u32[]{:S(2)}) collective-permute-start(bf16[1,1,8,2048]{3,2,0,1:T(8,128)(2,1)S(1)} %get-tuple-element.172), channel_id=1, source_target_pairs={{0,7},{1,8},{2,9},{3,10},{4,11},{5,12},{6,13},{7,14},{8,15},{9,0},... | collective-permute-start | bytes 98312 | tf_op jit(solution)/shard_map/ppermute | solution.py:26
  131.8 7.7 %collective-permute-start.7 = (bf16[1,1,8,2048]{3,2,0,1:T(8,128)(2,1)S(1)}, bf16[1,1,8,2048]{3,2,0,1:T(8,128)(2,1)S(1)}, u32[]{:S(2)}, u32[]{:S(2)}) collective-permute-start(bf16[1,1,8,2048]{3,2,0,1:T(8,128)(2,1)S(1)} %get-tuple-element.171), channel_id=1, source_target_pairs={{0,8},{1,9},{2,10},{3,11},{4,12},{5,13},{6,14},{7,15},{8,0},{9,1},... | collective-permute-start | bytes 98312 | tf_op jit(solution)/shard_map/ppermute | solution.py:26
  133.6 6.5 %collective-permute-start.8 = (bf16[1,1,8,2048]{3,2,0,1:T(8,128)(2,1)S(1)}, bf16[1,1,8,2048]{3,2,0,1:T(8,128)(2,1)S(1)}, u32[]{:S(2)}, u32[]{:S(2)}) collective-permute-start(bf16[1,1,8,2048]{3,2,0,1:T(8,128)(2,1)S(1)} %get-tuple-element.170), channel_id=1, source_target_pairs={{0,9},{1,10},{2,11},{3,12},{4,13},{5,14},{6,15},{7,0},{8,1},{9,2},... | collective-permute-start | bytes 98312 | tf_op jit(solution)/shard_map/ppermute | solution.py:26
  133.7 8.4 %collective-permute-start.9 = (bf16[1,1,8,2048]{3,2,0,1:T(8,128)(2,1)S(1)}, bf16[1,1,8,2048]{3,2,0,1:T(8,128)(2,1)S(1)}, u32[]{:S(2)}, u32[]{:S(2)}) collective-permute-start(bf16[1,1,8,2048]{3,2,0,1:T(8,128)(2,1)S(1)} %get-tuple-element.169), channel_id=1, source_target_pairs={{0,10},{1,11},{2,12},{3,13},{4,14},{5,15},{6,0},{7,1},{8,2},{9,3},... | collective-permute-start | bytes 98312 | tf_op jit(solution)/shard_map/ppermute | solution.py:26
  135.2 9.6 %collective-permute-start.10 = (bf16[1,1,8,2048]{3,2,0,1:T(8,128)(2,1)S(1)}, bf16[1,1,8,2048]{3,2,0,1:T(8,128)(2,1)S(1)}, u32[]{:S(2)}, u32[]{:S(2)}) collective-permute-start(bf16[1,1,8,2048]{3,2,0,1:T(8,128)(2,1)S(1)} %get-tuple-element.168), channel_id=1, source_target_pairs={{0,11},{1,12},{2,13},{3,14},{4,15},{5,0},{6,1},{7,2},{8,3},{9,4},{... | collective-permute-start | bytes 98312 | tf_op jit(solution)/shard_map/ppermute | solution.py:26
  138.7 6.1 %collective-permute-start.11 = (bf16[1,1,8,2048]{3,2,0,1:T(8,128)(2,1)S(1)}, bf16[1,1,8,2048]{3,2,0,1:T(8,128)(2,1)S(1)}, u32[]{:S(2)}, u32[]{:S(2)}) collective-permute-start(bf16[1,1,8,2048]{3,2,0,1:T(8,128)(2,1)S(1)} %get-tuple-element.167), channel_id=1, source_target_pairs={{0,12},{1,13},{2,14},{3,15},{4,0},{5,1},{6,2},{7,3},{8,4},{9,5},{1... | collective-permute-start | bytes 98312 | tf_op jit(solution)/shard_map/ppermute | solution.py:26
  139.5 5.4 %collective-permute-start.12 = (bf16[1,1,8,2048]{3,2,0,1:T(8,128)(2,1)S(1)}, bf16[1,1,8,2048]{3,2,0,1:T(8,128)(2,1)S(1)}, u32[]{:S(2)}, u32[]{:S(2)}) collective-permute-start(bf16[1,1,8,2048]{3,2,0,1:T(8,128)(2,1)S(1)} %get-tuple-element.166), channel_id=1, source_target_pairs={{0,13},{1,14},{2,15},{3,0},{4,1},{5,2},{6,3},{7,4},{8,5},{9,6},{10... | collective-permute-start | bytes 98312 | tf_op jit(solution)/shard_map/ppermute | solution.py:26
  140.1 4.8 %collective-permute-start.13 = (bf16[1,1,8,2048]{3,2,0,1:T(8,128)(2,1)S(1)}, bf16[1,1,8,2048]{3,2,0,1:T(8,128)(2,1)S(1)}, u32[]{:S(2)}, u32[]{:S(2)}) collective-permute-start(bf16[1,1,8,2048]{3,2,0,1:T(8,128)(2,1)S(1)} %get-tuple-element.165), channel_id=1, source_target_pairs={{0,14},{1,15},{2,0},{3,1},{4,2},{5,3},{6,4},{7,5},{8,6},{9,7},{10,... | collective-permute-start | bytes 98312 | tf_op jit(solution)/shard_map/ppermute | solution.py:26
  142.1 4.3 %collective-permute-start.14 = (bf16[1,1,8,2048]{3,2,0,1:T(8,128)(2,1)S(1)}, bf16[1,1,8,2048]{3,2,0,1:T(8,128)(2,1)S(1)}, u32[]{:S(2)}, u32[]{:S(2)}) collective-permute-start(bf16[1,1,8,2048]{3,2,0,1:T(8,128)(2,1)S(1)} %get-tuple-element.164), channel_id=1, source_target_pairs={{0,15},{1,0},{2,1},{3,2},{4,3},{5,4},{6,5},{7,6},{8,7},{9,8},{10,9... | collective-permute-start | bytes 98312 | tf_op jit(solution)/shard_map/ppermute | solution.py:26
  148.2 3.5 %copy-start.2 = (bf16[1024,2048]{1,0:T(8,128)(2,1)S(1)}, bf16[1024,2048]{1,0:T(8,128)(2,1)}, u32[]{:S(2)}) copy-start(bf16[1024,2048]{1,0:T(8,128)(2,1)} %param.26) | copy-start | bytes 12582916
  153.2 3.5 %copy-start.3 = (bf16[1024,2048]{1,0:T(8,128)(2,1)S(1)}, bf16[1024,2048]{1,0:T(8,128)(2,1)}, u32[]{:S(2)}) copy-start(bf16[1024,2048]{1,0:T(8,128)(2,1)} %param.26) | copy-start | bytes 12582916
  156.8 0.9 copy-start.6
  158.2 3.5 %copy-start.4 = (bf16[1024,2048]{1,0:T(8,128)(2,1)S(1)}, bf16[1024,2048]{1,0:T(8,128)(2,1)}, u32[]{:S(2)}) copy-start(bf16[1024,2048]{1,0:T(8,128)(2,1)} %param.26) | copy-start | bytes 12582916
  161.8 1.7 %copy-start.7 = (bf16[128,1024]{1,0:T(8,128)(2,1)S(1)}, bf16[128,1024]{1,0:T(8,128)(2,1)}, u32[]{:S(2)}) copy-start(bf16[128,1024]{1,0:T(8,128)(2,1)} %copy-done.6) | copy-start | bytes 786436
Sparse Core Ops, SparseCore 0:
  12.6 77.2 all-gather.3
